TPU v7x, 512 devices: a whole 4x4x16 slice. The times are simulated.
512 devices in a mesh: blk: 32 (over x, z_lo), rep: 16 (over z_hi, y, core).
Axes of the slice: x: 4, y: 4, z: 16 (z_hi: 2, z_lo: 8; z = z_hi * 8 + z_lo), core: 2. Of those that a mesh axis runs over, the one named last changes fastest.
Arguments:
- signals: bfloat16 [32768, 8192], P('rep', 'blk'), may hold values from -6 to 6
- omega: float32 [32, 5, 256, 256], P('blk', None, 'rep'), may hold values from -1.2 to 3, as said below
- pattern: int32 [32, 5], P('blk'), may hold values from 0 to 31, as said below
Outputs:
- omega_next: float32 [32, 5, 256, 256], P('blk', None, 'rep')
Inputs may be any that keep to these rules, and one draw needn't show every extreme that they name: pattern[i, 0] = i. For two distinct whole numbers A and B from 1 to 15, the same in every row, pattern[i, 1] to pattern[i, 4] are i + A, i - A, i + B and i - B modulo 32 in some order, the same order in every row. Omega is symmetric: omega[i, k] is the transpose of omega[pattern[i, k], k2] where pattern[pattern[i, k], k2] = i. The diagonal entries of omega[i, 0] lie between 1 and 3.
All inputs are finite; a program needn't handle non-finite values.
Results may differ from a plain program's by a relative error of at most 0.0033.
Values may be sent and summed in bfloat16 or wider, within the bound.
A program may use at most 128 MiB of HBM per device.

v0:
```python
import jax
import jax.numpy as jnp
from jax import lax
from jax.sharding import PartitionSpec as P

STEP_SIZE = 0.5
PENALTY = 0.1


def shifted_2(block, axis, distance):
    devices = range(lax.axis_size(axis))
    route = [((i - distance) % len(devices), i) for i in devices]
    return lax.ppermute(block, axis, route)


def advance(stacked, shifted, distance, section_index):
    chosen = jnp.mod(distance // (1 << section_index), 2) == 1
    return jnp.where(chosen[:, None, None], shifted, stacked)


def slot_order(drawn_offsets, team_count):
    slot_ids = jnp.arange(drawn_offsets.shape[0], dtype=jnp.int32)
    partner = jnp.argmax(drawn_offsets == team_count - drawn_offsets[1])
    third = jnp.where(partner == 2, 3, 2).astype(jnp.int32)
    fourth = jnp.where(partner == 4, 3, 4).astype(jnp.int32)
    order = jnp.stack([jnp.zeros((), jnp.int32), jnp.ones((), jnp.int32), partner, third, fourth])
    inverse = jnp.argmax(order[None, :] == slot_ids[:, None], axis=1)
    return (order, inverse)


def per_device(signals, omega, pattern):
    team_count = lax.axis_size("blk")
    replica_count = lax.axis_size("rep")
    level_count = team_count.bit_length() - 1
    team_index = lax.axis_index("blk")
    replica_index = lax.axis_index("rep")
    slot_count = omega.shape[1]
    tile_rows = omega.shape[2]
    tile_width = omega.shape[3]
    time_length = signals.shape[0] * replica_count
    drawn_offsets = jnp.mod(pattern[0] - team_index, team_count)
    order, inverse = slot_order(drawn_offsets, team_count)
    offsets = drawn_offsets[order]
    own_tiles = omega[0][order]
    panels = lax.all_gather(omega.astype(jnp.bfloat16), "rep", axis=2, tiled=True)[0][order]
    remote = jnp.broadcast_to(signals[None], (slot_count - 1,) + signals.shape)
    distance = offsets[1:]
    for section_index in range(level_count):
        shifted = shifted_2(remote, "blk", -(1 << section_index))
        remote = advance(remote, shifted, distance, section_index)
    gathered = jnp.concatenate([signals[None], remote], axis=0)
    mixed = jnp.einsum("ktc,kdc->td", gathered, panels, preferred_element_type=jnp.float32).astype(
        jnp.bfloat16
    )
    left_terms = jnp.einsum("td,ktc->kdc", mixed, gathered, preferred_element_type=jnp.float32)
    stacked = jnp.concatenate([left_terms, jnp.swapaxes(left_terms, 1, 2)], axis=0)
    first_row = replica_index * tile_rows
    summed = lax.psum(stacked, "rep")
    summed = lax.dynamic_slice_in_dim(summed, first_row, tile_rows, 1)
    own_terms = summed[:slot_count]
    flipped = summed[slot_count:]
    mirrored = [
        flipped[slot_index + 1] if slot_index % 2 == 1 else flipped[slot_index - 1]
        for slot_index in range(1, slot_count)
    ]
    outgoing = jnp.stack(mirrored)
    distance = offsets[1:]
    for section_index in range(level_count):
        shifted = shifted_2(outgoing, "blk", -(1 << section_index))
        outgoing = advance(outgoing, shifted, distance, section_index)
    returned = jnp.concatenate([flipped[0:1], outgoing], axis=0)
    gradient = (own_terms + returned) / (2.0 * time_length)
    column_ids = jnp.arange(tile_width, dtype=jnp.int32)
    row_ids = first_row + jnp.arange(tile_rows, dtype=jnp.int32)
    diagonal_mask = column_ids[None, :] == row_ids[:, None]
    diag_values = jnp.sum(jnp.where(diagonal_mask, own_tiles[0], 0.0), axis=1)
    first_grad = gradient[0] - jnp.where(diagonal_mask, (1.0 / diag_values)[:, None], 0.0)
    gradient = jnp.concatenate([first_grad[None], gradient[1:]], axis=0)
    updated = own_tiles - STEP_SIZE * gradient
    shrunk = jnp.sign(updated) * jnp.maximum(jnp.abs(updated) - STEP_SIZE * PENALTY, 0.0)
    slot_ids = jnp.arange(slot_count, dtype=jnp.int32)
    keep_mask = (slot_ids[:, None, None] == 0) & diagonal_mask[None]
    result = jnp.where(keep_mask, updated, shrunk)
    return result[inverse][None]


def solution(mesh):
    return jax.shard_map(
        per_device,
        mesh=mesh,
        in_specs=(P("rep", "blk"), P("blk", None, "rep", None), P("blk", None)),
        out_specs=P("blk", None, "rep", None),
        check_vma=False,
    )
```

profile of v0, /device:TPU:230, one launch (start us, length us, event | category | flops | bytes accessed | tf_op | source)
XLA Modules:
  0.0 1216.6 jit_solution(44980131006456918)
XLA Ops:
  6.5 3.5 broadcast_in_dim.114
  10.1 2.0 collective-permute-start
  16.6 96.7 %collective-permute-done = bf16[4,2048,256]{2,1,0:T(8,128)(2,1)} collective-permute-done((bf16[4,2048,256]{2,1,0:T(8,128)(2,1)}, bf16[4,2048,256]{2,1,0:T(8,128)(2,1)}, u32[]{:S(2)}, u32[]{:S(2)}) %collective-permute-start) | collective-permute-done | bytes 4194336 | tf_op jit(solution)/shard_map/ppermute | solution.py:13
  113.3 2.8 broadcast_select_fusion
  116.1 1.9 collective-permute-start.1
  118.0 180.3 %collective-permute-done.1 = bf16[4,2048,256]{2,1,0:T(8,128)(2,1)S(1)} collective-permute-done((bf16[4,2048,256]{2,1,0:T(8,128)(2,1)S(1)}, bf16[4,2048,256]{2,1,0:T(8,128)(2,1)S(1)}, u32[]{:S(2)}, u32[]{:S(2)}) %collective-permute-start.1) | collective-permute-done | bytes 4194336 | tf_op jit(solution)/shard_map/ppermute | solution.py:13
  298.3 2.8 broadcast_select_fusion.1
  301.1 1.9 collective-permute-start.2
  303.0 356.7 %collective-permute-done.2 = bf16[4,2048,256]{2,1,0:T(8,128)(2,1)S(1)} collective-permute-done((bf16[4,2048,256]{2,1,0:T(8,128)(2,1)S(1)}, bf16[4,2048,256]{2,1,0:T(8,128)(2,1)S(1)}, u32[]{:S(2)}, u32[]{:S(2)}) %collective-permute-start.2) | collective-permute-done | bytes 4194336 | tf_op jit(solution)/shard_map/ppermute | solution.py:13
  660.3 1.9 collective-permute-start.3
  662.2 93.7 %collective-permute-done.3 = bf16[4,2048,256]{2,1,0:T(8,128)(2,1)S(1)} collective-permute-done((bf16[4,2048,256]{2,1,0:T(8,128)(2,1)S(1)}, bf16[4,2048,256]{2,1,0:T(8,128)(2,1)S(1)}, u32[]{:S(2)}, u32[]{:S(2)}) %collective-permute-start.3) | collective-permute-done | bytes 4194336 | tf_op jit(solution)/shard_map/ppermute | solution.py:13
  755.9 2.4 broadcast_select_fusion.3
  760.2 45.1 %all_gather.3 = bf16[1,5,256,256]{3,2,1,0:T(8,128)(2,1)S(1)} all-gather(bf16[1,5,16,256]{3,2,1,0:T(8,128)(2,1)S(1)} %convert_element_type.6), channel_id=1, replica_groups=mesh['blk'=32,'rep'=16] {'rep'}, dimensions={2}, use_global_device_ids=true | all-gather | bytes 696320 | tf_op jit(solution)/shard_map/all_gather | solution.py:45
  805.9 47.7 %collective-permute-done.4 = bf16[4,2048,256]{2,1,0:T(8,128)(2,1)} collective-permute-done((bf16[4,2048,256]{2,1,0:T(8,128)(2,1)}, bf16[4,2048,256]{2,1,0:T(8,128)(2,1)}, u32[]{:S(2)}, u32[]{:S(2)}) %collective-permute-start.4) | collective-permute-done | bytes 4194336 | tf_op jit(solution)/shard_map/ppermute | solution.py:13
  853.7 4.0 broadcast_select_fusion.4
  862.5 3.0 pad_maximum_fusion.5
  867.4 282.8 %all-reduce.2.cloned.1.call-done = f32[10,256,256]{2,1,0:T(8,128)} async-done(((f32[10,256,256]{2,1,0:T(8,128)}), f32[10,256,256]{2,1,0:T(8,128)}) %all-reduce.2.cloned.1.call-update) | async-done | bytes 2621456 | tf_op jit(solution)/shard_map/psum | solution.py:58
  1151.0 2.0 collective-permute-start.5
  1153.2 12.7 %collective-permute-done.5 = f32[4,16,256]{2,1,0:T(8,128)S(1)} collective-permute-done((f32[4,16,256]{2,1,0:T(8,128)S(1)}, f32[4,16,256]{2,1,0:T(8,128)S(1)}, u32[]{:S(2)}, u32[]{:S(2)}) %collective-permute-start.5) | collective-permute-done | bytes 65568 | tf_op jit(solution)/shard_map/ppermute | solution.py:13
  1167.9 12.1 collective-permute-done.6
  1180.1 1.9 collective-permute-start.7
  1182.1 10.2 collective-permute-done.7
  1194.3 5.4 collective-permute-done.8
  1201.7 5.7 collective-permute-done.9
  (48 shorter events, 21.8 us)
Async XLA Ops:
  6.5 106.8 %copy-start = (bf16[2048,256]{1,0:T(8,128)(2,1)S(1)}, bf16[2048,256]{1,0:T(8,128)(2,1)}, u32[]{:S(2)}) copy-start(bf16[2048,256]{1,0:T(8,128)(2,1)} %param.3) | copy-start | bytes 3145732
  6.5 5.5 copy-start.2
  6.5 1143.7 %all-reduce.2.cloned.1.call-start = ((), (), s32[]{:S(2)}) async-start(), calls=%async_computation | async-start | bytes 5242880 | tf_op jit(solution)/shard_map/psum | solution.py:58
  10.1 103.2 %collective-permute-start = (bf16[4,2048,256]{2,1,0:T(8,128)(2,1)}, bf16[4,2048,256]{2,1,0:T(8,128)(2,1)}, u32[]{:S(2)}, u32[]{:S(2)}) collective-permute-start(bf16[4,2048,256]{2,1,0:T(8,128)(2,1)} %broadcast_in_dim.114), channel_id=1, source_target_pairs={{16,0},{32,16},{48,32},{64,48},{80,64},{96,80},{112,96},{128,112},... | collective-permute-start | bytes 12582920 | tf_op jit(solution)/shard_map/ppermute | solution.py:13
  116.1 182.3 %collective-permute-start.1 = (bf16[4,2048,256]{2,1,0:T(8,128)(2,1)S(1)}, bf16[4,2048,256]{2,1,0:T(8,128)(2,1)S(1)}, u32[]{:S(2)}, u32[]{:S(2)}) collective-permute-start(bf16[4,2048,256]{2,1,0:T(8,128)(2,1)S(1)} %broadcast_select_fusion), channel_id=1, source_target_pairs={{32,0},{48,16},{64,32},{80,48},{96,64},{112,80},{128,96},{144,112}... | collective-permute-start | bytes 12582920 | tf_op jit(solution)/shard_map/ppermute | solution.py:13
  301.1 358.7 %collective-permute-start.2 = (bf16[4,2048,256]{2,1,0:T(8,128)(2,1)S(1)}, bf16[4,2048,256]{2,1,0:T(8,128)(2,1)S(1)}, u32[]{:S(2)}, u32[]{:S(2)}) collective-permute-start(bf16[4,2048,256]{2,1,0:T(8,128)(2,1)S(1)} %broadcast_select_fusion.1), channel_id=1, source_target_pairs={{64,0},{80,16},{96,32},{112,48},{128,64},{144,80},{160,96},{176,11... | collective-permute-start | bytes 12582920 | tf_op jit(solution)/shard_map/ppermute | solution.py:13
  660.3 95.6 %collective-permute-start.3 = (bf16[4,2048,256]{2,1,0:T(8,128)(2,1)S(1)}, bf16[4,2048,256]{2,1,0:T(8,128)(2,1)S(1)}, u32[]{:S(2)}, u32[]{:S(2)}) collective-permute-start(bf16[4,2048,256]{2,1,0:T(8,128)(2,1)S(1)} %broadcast_select_fusion.2), channel_id=1, source_target_pairs={{128,0},{144,16},{160,32},{176,48},{192,64},{208,80},{224,96},{240... | collective-permute-start | bytes 12582920 | tf_op jit(solution)/shard_map/ppermute | solution.py:13
  755.9 4.3 copy-start.1
  758.3 95.4 %collective-permute-start.4 = (bf16[4,2048,256]{2,1,0:T(8,128)(2,1)}, bf16[4,2048,256]{2,1,0:T(8,128)(2,1)}, u32[]{:S(2)}, u32[]{:S(2)}) collective-permute-start(bf16[4,2048,256]{2,1,0:T(8,128)(2,1)} %broadcast_select_fusion.3), channel_id=1, source_target_pairs={{256,0},{272,16},{288,32},{304,48},{320,64},{336,80},{352,96},{368... | collective-permute-start | bytes 12582920 | tf_op jit(solution)/shard_map/ppermute | solution.py:13
  1151.0 14.9 %collective-permute-start.5 = (f32[4,16,256]{2,1,0:T(8,128)S(1)}, f32[4,16,256]{2,1,0:T(8,128)S(1)}, u32[]{:S(2)}, u32[]{:S(2)}) collective-permute-start(f32[4,16,256]{2,1,0:T(8,128)S(1)} %pad_maximum_fusion.10), channel_id=1, source_target_pairs={{16,0},{32,16},{48,32},{64,48},{80,64},{96,80},{112,96},{128,112},... | collective-permute-start | bytes 196616 | tf_op jit(solution)/shard_map/ppermute | solution.py:13
  1166.0 14.1 %collective-permute-start.6 = (f32[4,16,256]{2,1,0:T(8,128)S(1)}, f32[4,16,256]{2,1,0:T(8,128)S(1)}, u32[]{:S(2)}, u32[]{:S(2)}) collective-permute-start(f32[4,16,256]{2,1,0:T(8,128)S(1)} %broadcast_select_fusion.5), channel_id=1, source_target_pairs={{32,0},{48,16},{64,32},{80,48},{96,64},{112,80},{128,96},{144,112}... | collective-permute-start | bytes 196616 | tf_op jit(solution)/shard_map/ppermute | solution.py:13
  1180.1 12.2 %collective-permute-start.7 = (f32[4,16,256]{2,1,0:T(8,128)S(1)}, f32[4,16,256]{2,1,0:T(8,128)S(1)}, u32[]{:S(2)}, u32[]{:S(2)}) collective-permute-start(f32[4,16,256]{2,1,0:T(8,128)S(1)} %broadcast_select_fusion.6), channel_id=1, source_target_pairs={{64,0},{80,16},{96,32},{112,48},{128,64},{144,80},{160,96},{176,11... | collective-permute-start | bytes 196616 | tf_op jit(solution)/shard_map/ppermute | solution.py:13
  1192.4 7.4 collective-permute-start.8
  1199.8 7.7 collective-permute-start.9
Sparse Core Ops, SparseCore 0:
  865.6 284.5 all-reduce.1
where the time goes:
time: 1220 us
  waiting for transfers between devices  1100 us (90%)
  blocking collectives  45.1 us (4%)
  starting transfers between devices  19.3 us (2%)
  other arithmetic  18.6 us (2%)
  between operations  15.4 us (1%)
    ppermute x10, waiting for transfers between devices, shifted_2(): return lax.ppermute(block, axis, route)  821 us
    psum x1, waiting for transfers between devices, per_device(): summed = lax.psum(stacked, 'rep')  283 us
    all_gather x1, blocking collectives, per_device(): lax.all_gather(omega.astype(jnp.bfloat16), 'rep', axis=2, tiled=True)[0]  45.1 us
  transfers between devices with their start and end apart: 11, of which 11 were waited for; matrix products, arithmetic and copies ran while one was open for 0% of the time, Pallas kernels for 0%

commit v1 on v0

--- a/solution.py
+++ b/solution.py
@@ -55,7 +55,7 @@
     left_terms = jnp.einsum("td,ktc->kdc", mixed, gathered, preferred_element_type=jnp.float32)
     stacked = jnp.concatenate([left_terms, jnp.swapaxes(left_terms, 1, 2)], axis=0)
     first_row = replica_index * tile_rows
-    summed = lax.psum(stacked, "rep")
+    summed = jnp.sum(lax.all_gather(stacked, "rep"), axis=0)
     summed = lax.dynamic_slice_in_dim(summed, first_row, tile_rows, 1)
     own_terms = summed[:slot_count]
     flipped = summed[slot_count:]

time: 1220 us -> 1610 us (1.32)
  the two profiles are of different devices: /device:TPU:230 before, /device:TPU:38 now
where the time goes in v1:
time: 1610 us
  waiting for transfers between devices  1360 us (84%)
  starting transfers between devices  139 us (9%)
  blocking collectives  48.3 us (3%)
  other arithmetic  32.7 us (2%)
    ppermute x10, waiting for transfers between devices, shifted_2(): return lax.ppermute(block, axis, route)  728 us
    all_gather x1, waiting for transfers between devices, per_device(): summed = jnp.sum(lax.all_gather(stacked, 'rep'), axis=0)  631 us
    ppermute x10, starting transfers between devices, shifted_2(): return lax.ppermute(block, axis, route)  139 us
    all_gather x1, blocking collectives, per_device(): lax.all_gather(omega.astype(jnp.bfloat16), 'rep', axis=2, tiled=True)[0]  48.3 us
  transfers between devices with their start and end apart: 11, of which 11 were waited for; matrix products, arithmetic and copies ran while one was open for 0% of the time, Pallas kernels for 0%

profile of v1, /device:TPU:38, one launch (start us, length us, event | category | flops | bytes accessed | tf_op | source)
XLA Modules:
  0.0 1607.3 jit_solution(8769989886391807747)
XLA Ops:
  6.5 3.5 broadcast_in_dim.114
  16.8 87.9 %collective-permute-done = bf16[4,2048,256]{2,1,0:T(8,128)(2,1)} collective-permute-done((bf16[4,2048,256]{2,1,0:T(8,128)(2,1)}, bf16[4,2048,256]{2,1,0:T(8,128)(2,1)}, u32[]{:S(2)}, u32[]{:S(2)}) %collective-permute-start) | collective-permute-done | bytes 4194336 | tf_op jit(solution)/shard_map/ppermute | solution.py:13
  104.8 2.7 broadcast_select_fusion
  107.4 19.4 %collective-permute-start.1 = (bf16[4,2048,256]{2,1,0:T(8,128)(2,1)S(1)}, bf16[4,2048,256]{2,1,0:T(8,128)(2,1)S(1)}, u32[]{:S(2)}, u32[]{:S(2)}) collective-permute-start(bf16[4,2048,256]{2,1,0:T(8,128)(2,1)S(1)} %broadcast_select_fusion), channel_id=1, source_target_pairs={{32,0},{48,16},{64,32},{80,48},{96,64},{112,80},{128,96},{144,112}... | collective-permute-start | bytes 12582920 | tf_op jit(solution)/shard_map/ppermute | solution.py:13
  126.8 171.3 %collective-permute-done.1 = bf16[4,2048,256]{2,1,0:T(8,128)(2,1)S(1)} collective-permute-done((bf16[4,2048,256]{2,1,0:T(8,128)(2,1)S(1)}, bf16[4,2048,256]{2,1,0:T(8,128)(2,1)S(1)}, u32[]{:S(2)}, u32[]{:S(2)}) %collective-permute-start.1) | collective-permute-done | bytes 4194336 | tf_op jit(solution)/shard_map/ppermute | solution.py:13
  298.1 2.9 broadcast_select_fusion.1
  302.9 271.9 %collective-permute-done.2 = bf16[4,2048,256]{2,1,0:T(8,128)(2,1)S(1)} collective-permute-done((bf16[4,2048,256]{2,1,0:T(8,128)(2,1)S(1)}, bf16[4,2048,256]{2,1,0:T(8,128)(2,1)S(1)}, u32[]{:S(2)}, u32[]{:S(2)}) %collective-permute-start.2) | collective-permute-done | bytes 4194336 | tf_op jit(solution)/shard_map/ppermute | solution.py:13
  575.3 2.5 collective-permute-start.3
  577.8 93.0 %collective-permute-done.3 = bf16[4,2048,256]{2,1,0:T(8,128)(2,1)S(1)} collective-permute-done((bf16[4,2048,256]{2,1,0:T(8,128)(2,1)S(1)}, bf16[4,2048,256]{2,1,0:T(8,128)(2,1)S(1)}, u32[]{:S(2)}, u32[]{:S(2)}) %collective-permute-start.3) | collective-permute-done | bytes 4194336 | tf_op jit(solution)/shard_map/ppermute | solution.py:13
  670.8 2.4 broadcast_select_fusion.3
  675.4 48.3 %all_gather.9 = bf16[1,5,256,256]{3,2,1,0:T(8,128)(2,1)S(1)} all-gather(bf16[1,5,16,256]{3,2,1,0:T(8,128)(2,1)S(1)} %convert_element_type.6), channel_id=1, replica_groups=mesh['blk'=32,'rep'=16] {'rep'}, dimensions={2}, use_global_device_ids=true | all-gather | bytes 696320 | tf_op jit(solution)/shard_map/all_gather | solution.py:45
  724.3 44.2 %collective-permute-done.4 = bf16[4,2048,256]{2,1,0:T(8,128)(2,1)} collective-permute-done((bf16[4,2048,256]{2,1,0:T(8,128)(2,1)}, bf16[4,2048,256]{2,1,0:T(8,128)(2,1)}, u32[]{:S(2)}, u32[]{:S(2)}) %collective-permute-start.4) | collective-permute-done | bytes 4194336 | tf_op jit(solution)/shard_map/ppermute | solution.py:13
  768.6 4.0 broadcast_select_fusion.4
  777.3 3.1 pad_maximum_fusion.5
  782.4 630.9 %all-gather.3.cloned.1.call-done = f32[160,256,256]{2,1,0:T(8,128)} async-done(((f32[10,256,256]{2,1,0:T(8,128)}), f32[160,256,256]{2,1,0:T(8,128)}) %all-gather.3.cloned.1.call-update) | async-done | bytes 41943056 | tf_op jit(solution)/shard_map/all_gather | solution.py:58
  1413.3 14.8 reduce_sum.18
  1428.2 100.6 %collective-permute-start.5 = (f32[4,16,256]{2,1,0:T(8,128)S(1)}, f32[4,16,256]{2,1,0:T(8,128)S(1)}, u32[]{:S(2)}, u32[]{:S(2)}) collective-permute-start(f32[4,16,256]{2,1,0:T(8,128)S(1)} %pad_maximum_fusion.10), channel_id=1, source_target_pairs={{16,0},{32,16},{48,32},{64,48},{80,64},{96,80},{112,96},{128,112},... | collective-permute-start | bytes 196616 | tf_op jit(solution)/shard_map/ppermute | solution.py:13
  1529.0 15.1 collective-permute-done.5
  1546.1 25.7 %collective-permute-done.6 = f32[4,16,256]{2,1,0:T(8,128)S(1)} collective-permute-done((f32[4,16,256]{2,1,0:T(8,128)S(1)}, f32[4,16,256]{2,1,0:T(8,128)S(1)}, u32[]{:S(2)}, u32[]{:S(2)}) %collective-permute-start.6) | collective-permute-done | bytes 65568 | tf_op jit(solution)/shard_map/ppermute | solution.py:13
  1571.9 4.0 collective-permute-start.7
  1575.9 7.3 collective-permute-done.7
  1583.3 2.5 collective-permute-start.8
  1585.8 5.6 collective-permute-done.8
  1593.3 5.7 collective-permute-done.9
  (49 shorter events, 22.5 us)
Async XLA Ops:
  6.5 98.2 %copy-start = (bf16[2048,256]{1,0:T(8,128)(2,1)S(1)}, bf16[2048,256]{1,0:T(8,128)(2,1)}, u32[]{:S(2)}) copy-start(bf16[2048,256]{1,0:T(8,128)(2,1)} %param.3) | copy-start | bytes 3145732
  6.5 5.5 copy-start.2
  6.5 1406.8 %all-gather.3.cloned.1.call-start = ((), (), s32[]{:S(2)}) async-start(), calls=%async_computation | async-start | bytes 44564480 | tf_op jit(solution)/shard_map/all_gather | solution.py:58
  10.1 94.7 %collective-permute-start = (bf16[4,2048,256]{2,1,0:T(8,128)(2,1)}, bf16[4,2048,256]{2,1,0:T(8,128)(2,1)}, u32[]{:S(2)}, u32[]{:S(2)}) collective-permute-start(bf16[4,2048,256]{2,1,0:T(8,128)(2,1)} %broadcast_in_dim.114), channel_id=1, source_target_pairs={{16,0},{32,16},{48,32},{64,48},{80,64},{96,80},{112,96},{128,112},... | collective-permute-start | bytes 12582920 | tf_op jit(solution)/shard_map/ppermute | solution.py:13
  107.4 190.7 %collective-permute-start.1 = (bf16[4,2048,256]{2,1,0:T(8,128)(2,1)S(1)}, bf16[4,2048,256]{2,1,0:T(8,128)(2,1)S(1)}, u32[]{:S(2)}, u32[]{:S(2)}) collective-permute-start(bf16[4,2048,256]{2,1,0:T(8,128)(2,1)S(1)} %broadcast_select_fusion), channel_id=1, source_target_pairs={{32,0},{48,16},{64,32},{80,48},{96,64},{112,80},{128,96},{144,112}... | collective-permute-start | bytes 12582920 | tf_op jit(solution)/shard_map/ppermute | solution.py:13
  301.0 273.8 %collective-permute-start.2 = (bf16[4,2048,256]{2,1,0:T(8,128)(2,1)S(1)}, bf16[4,2048,256]{2,1,0:T(8,128)(2,1)S(1)}, u32[]{:S(2)}, u32[]{:S(2)}) collective-permute-start(bf16[4,2048,256]{2,1,0:T(8,128)(2,1)S(1)} %broadcast_select_fusion.1), channel_id=1, source_target_pairs={{64,0},{80,16},{96,32},{112,48},{128,64},{144,80},{160,96},{176,11... | collective-permute-start | bytes 12582920 | tf_op jit(solution)/shard_map/ppermute | solution.py:13
  575.3 95.5 %collective-permute-start.3 = (bf16[4,2048,256]{2,1,0:T(8,128)(2,1)S(1)}, bf16[4,2048,256]{2,1,0:T(8,128)(2,1)S(1)}, u32[]{:S(2)}, u32[]{:S(2)}) collective-permute-start(bf16[4,2048,256]{2,1,0:T(8,128)(2,1)S(1)} %broadcast_select_fusion.2), channel_id=1, source_target_pairs={{128,0},{144,16},{160,32},{176,48},{192,64},{208,80},{224,96},{240... | collective-permute-start | bytes 12582920 | tf_op jit(solution)/shard_map/ppermute | solution.py:13
  670.8 4.5 copy-start.1
  673.3 95.3 %collective-permute-start.4 = (bf16[4,2048,256]{2,1,0:T(8,128)(2,1)}, bf16[4,2048,256]{2,1,0:T(8,128)(2,1)}, u32[]{:S(2)}, u32[]{:S(2)}) collective-permute-start(bf16[4,2048,256]{2,1,0:T(8,128)(2,1)} %broadcast_select_fusion.3), channel_id=1, source_target_pairs={{256,0},{272,16},{288,32},{304,48},{320,64},{336,80},{352,96},{368... | collective-permute-start | bytes 12582920 | tf_op jit(solution)/shard_map/ppermute | solution.py:13
  1428.2 115.9 %collective-permute-start.5 = (f32[4,16,256]{2,1,0:T(8,128)S(1)}, f32[4,16,256]{2,1,0:T(8,128)S(1)}, u32[]{:S(2)}, u32[]{:S(2)}) collective-permute-start(f32[4,16,256]{2,1,0:T(8,128)S(1)} %pad_maximum_fusion.10), channel_id=1, source_target_pairs={{16,0},{32,16},{48,32},{64,48},{80,64},{96,80},{112,96},{128,112},... | collective-permute-start | bytes 196616 | tf_op jit(solution)/shard_map/ppermute | solution.py:13
  1544.2 27.7 %collective-permute-start.6 = (f32[4,16,256]{2,1,0:T(8,128)S(1)}, f32[4,16,256]{2,1,0:T(8,128)S(1)}, u32[]{:S(2)}, u32[]{:S(2)}) collective-permute-start(f32[4,16,256]{2,1,0:T(8,128)S(1)} %broadcast_select_fusion.5), channel_id=1, source_target_pairs={{32,0},{48,16},{64,32},{80,48},{96,64},{112,80},{128,96},{144,112}... | collective-permute-start | bytes 196616 | tf_op jit(solution)/shard_map/ppermute | solution.py:13
  1571.9 11.3 collective-permute-start.7
  1583.3 8.1 collective-permute-start.8
  1591.4 7.7 collective-permute-start.9
Sparse Core Ops, SparseCore 0:
  780.5 632.7 all-gather.2
